TPU v7x, 512 devices: a whole 4x8x8 slice. The times are simulated.
512 devices in a mesh: row: 16 (over y, core), col: 32 (over z, x).
Axes of the slice: x: 4, y: 8, z: 8, core: 2. Of those that a mesh axis runs over, the one named last changes fastest.
Arguments:
- query_matrix: bfloat16 [128, 512, 768], P('row', 'col'), may hold values from -6 to 16.133757
- key_matrix: bfloat16 [128, 512, 768], P('row', 'col'), may hold values from -6 to 6
- value_matrix: bfloat16 [128, 512, 768], P('row', 'col'), may hold values from -6 to 6
- tissue: int32 [128, 512], replicated, may hold values 0 or 1
- dilation_levels: int32 [16], replicated, may hold values from 0 to 2
- segment_levels: int32 [16], replicated, may hold values from 0 to 2
- output_matrix: bfloat16 [768, 768], replicated, may hold values from -0.21875 to 0.21875
Outputs:
- encoded: bfloat16 [128, 512, 768], P('row', 'col')
Inputs may be any that keep to these rules, and one draw needn't show every extreme that they name: 1 marks a tissue tile, 0 background. Head h uses the dilation 8 * 2^dilation_levels[h]. Head h uses segments of 512 / 2^segment_levels[h] tiles of a grid row.
All inputs are finite; a program needn't handle non-finite values.
Results may differ from a plain program's by a relative error of at most 0.0055.
Values may be sent and summed in bfloat16 or wider, within the bound.
No kernel may reach another device: no remote copies, remote signals or barrier semaphores. Data moves between devices by JAX's collectives and lax.ppermute only.
A program may use at most 64 MiB of HBM per device.

v0:
```python
import math
import jax
import jax.numpy as jnp
import numpy as np
from jax import lax
from jax.sharding import PartitionSpec as P

HEAD_COUNT = 16
R = 8
DILATION_MIN = 8
NEG_FILL = -1e30


def padded_2(x, sides, width):
    for axis, dim in sides:
        peers, length = (lax.axis_size(axis), x.shape[dim])
        up = [(i, (i + 1) % peers) for i in range(peers - 1)]
        down = [(j, i) for i, j in up]
        last = lax.slice_in_dim(x, length - width, length, axis=dim)
        first = lax.slice_in_dim(x, 0, width, axis=dim)
        before = lax.ppermute(last, axis, up)
        after = lax.ppermute(first, axis, down)
        x = jnp.concatenate([before, x, after], axis=dim)
    return x


def window_static(device_rows, device_columns):
    region_rows = np.arange(device_rows + 2 * R) - R
    query_rows = np.arange(device_rows)
    region_cols = np.arange(device_columns + 2 * R) - R
    query_cols = np.arange(device_columns)
    near_rows = np.abs(region_rows[None, :] - query_rows[:, None]) <= R
    near_cols = np.abs(region_cols[None, :] - query_cols[:, None]) <= R
    same_rows = region_rows[None, :] == query_rows[:, None]
    same_cols = region_cols[None, :] == query_cols[:, None]
    near_both = near_rows[:, None, :, None] & near_cols[None, :, None, :]
    self_both = same_rows[:, None, :, None] & same_cols[None, :, None, :]
    return (near_both, self_both)


def window_part(queries, key_region, value_region, permitted_mask, group_size):
    head_dimension = queries.shape[-1] // HEAD_COUNT
    scale = 1.0 / math.sqrt(head_dimension)
    numerators, maxima, totals = ([], [], [])
    for head_first in range(0, HEAD_COUNT, group_size):
        lower = head_first * head_dimension
        upper = (head_first + group_size) * head_dimension
        query_grp = queries[:, lower:upper].reshape(queries.shape[0], group_size, head_dimension)
        key_grp = key_region[:, lower:upper].reshape(
            key_region.shape[0], group_size, head_dimension
        )
        value_grp = value_region[:, lower:upper].reshape(
            value_region.shape[0], group_size, head_dimension
        )
        scores = (
            jnp.einsum("qhd,khd->hqk", query_grp, key_grp, preferred_element_type=jnp.float32)
            * scale
        )
        scores = jnp.where(permitted_mask[None], scores, NEG_FILL)
        highest = jnp.max(scores, axis=-1)
        exp_terms = jnp.exp(scores - highest[..., None])
        totals.append(jnp.sum(exp_terms, axis=-1))
        numerators.append(
            jnp.einsum(
                "hqk,khd->qhd",
                exp_terms.astype(jnp.bfloat16),
                value_grp,
                preferred_element_type=jnp.float32,
            )
        )
        maxima.append(highest)
    return (
        jnp.concatenate(numerators, axis=1),
        jnp.concatenate(maxima, axis=0).T,
        jnp.concatenate(totals, axis=0).T,
    )


def dilation_valid_mask(
    tissue,
    row_indices,
    head_indices,
    column_indices,
    dilation_levels,
    segment_levels,
    selected_count,
    column_total,
):
    key_columns = (
        jnp.arange(selected_count, dtype=jnp.int32)[None, :] * DILATION_MIN
        + (head_indices % DILATION_MIN)[:, None]
    )
    tissue_keys = tissue[row_indices[:, None], key_columns]
    dilation_stride = jnp.left_shift(jnp.int32(DILATION_MIN), dilation_levels[head_indices])
    segment = jnp.right_shift(jnp.int32(column_total), segment_levels[head_indices])
    phase_ok = key_columns % dilation_stride[:, None] == (head_indices % dilation_stride)[:, None]
    key_seg = key_columns // segment[:, None]
    query_seg = column_indices[None, :] // segment[:, None]
    same_seg = key_seg[:, None, :] == query_seg[:, :, None]
    return same_seg & ((tissue_keys == 1) & phase_ok)[:, None, :]


def dilation_in_grid(queries, keys_sel, values_sel, permitted_mask):
    scale = 1.0 / math.sqrt(queries.shape[-1])
    scores = (
        jnp.einsum("rchw,rshw->rhcs", queries, keys_sel, preferred_element_type=jnp.float32) * scale
    )
    scores = jnp.where(permitted_mask, scores, NEG_FILL)
    highest = jnp.max(scores, axis=-1)
    exp_terms = jnp.where(permitted_mask, jnp.exp(scores - highest[..., None]), 0.0)
    totals = jnp.sum(exp_terms, axis=-1)
    softmax_numer = jnp.einsum(
        "rhcs,rshw->rchw",
        exp_terms.astype(jnp.bfloat16),
        values_sel,
        preferred_element_type=jnp.float32,
    )
    return (softmax_numer, highest, totals)


def merge_partials(
    neighbour_numer, neighbour_max, neighbour_sum, dilation_numer, dilation_score_max, dilation_sum
):
    running_maximum = jnp.maximum(neighbour_max, dilation_score_max)
    neighbour_rescale = jnp.exp(neighbour_max - running_maximum)
    dilation_rescale = jnp.exp(dilation_score_max - running_maximum)
    softmax_numer = (
        neighbour_rescale[..., None] * neighbour_numer
        + dilation_rescale[..., None] * dilation_numer
    )
    softmax_denom = neighbour_rescale * neighbour_sum + dilation_rescale * dilation_sum
    return softmax_numer / softmax_denom[..., None]


def per_device(
    query_matrix, key_matrix, value_matrix, tissue, dilation_levels, segment_levels, output_matrix
):
    device_rows, device_columns, model_width = query_matrix.shape
    head_dimension = model_width // HEAD_COUNT
    col_count = lax.axis_size("col")
    column_total = device_columns * col_count
    selected_count = column_total // DILATION_MIN
    local_selection = device_columns // DILATION_MIN
    row_offset = lax.axis_index("row") * device_rows
    column_offset = lax.axis_index("col") * device_columns
    packed = jnp.concatenate([key_matrix, value_matrix], axis=-1)
    padded = padded_2(packed, (("row", 0), ("col", 1)), R)
    key_region = padded[:, :, :model_width].reshape(-1, model_width)
    value_region = padded[:, :, model_width:].reshape(-1, model_width)
    tissue_pad = jnp.pad(tissue, R)
    tissue_reg = lax.dynamic_slice(
        tissue_pad, (row_offset, column_offset), (device_rows + 2 * R, device_columns + 2 * R)
    )
    near_both, self_both = window_static(device_rows, device_columns)
    permitted_mask = jnp.asarray(near_both) & (tissue_reg[None, None] == 1) | jnp.asarray(self_both)
    permitted_mask = permitted_mask.reshape(device_rows * device_columns, -1)
    neighbour_numer, neighbour_max, neighbour_sum = window_part(
        query_matrix.reshape(-1, model_width), key_region, value_region, permitted_mask, 2
    )
    phase_table = np.arange(HEAD_COUNT)[None, :] % DILATION_MIN == np.arange(DILATION_MIN)[:, None]
    phase_table = jnp.asarray(phase_table)[None, None, :, :, None]
    key_phases = key_matrix.reshape(
        device_rows, local_selection, DILATION_MIN, HEAD_COUNT, head_dimension
    )
    value_phases = value_matrix.reshape(
        device_rows, local_selection, DILATION_MIN, HEAD_COUNT, head_dimension
    )
    zero_entry = jnp.zeros((), jnp.bfloat16)
    key_selected = jnp.sum(
        jnp.where(phase_table, key_phases, zero_entry), axis=2, dtype=jnp.bfloat16
    ).reshape(device_rows, local_selection, model_width)
    value_selected = jnp.sum(
        jnp.where(phase_table, value_phases, zero_entry), axis=2, dtype=jnp.bfloat16
    ).reshape(device_rows, local_selection, model_width)
    token_count = device_rows * HEAD_COUNT
    k_all, v_all = (
        lax.all_gather(key_selected, "col", axis=1, tiled=True),
        lax.all_gather(value_selected, "col", axis=1, tiled=True),
    )
    key_grid = k_all.reshape(device_rows, selected_count, HEAD_COUNT, head_dimension)
    value_grid = v_all.reshape(device_rows, selected_count, HEAD_COUNT, head_dimension)
    item_ids = jnp.arange(token_count, dtype=jnp.int32)
    column_indices = column_offset + jnp.arange(device_columns, dtype=jnp.int32)
    dilation_permitted = dilation_valid_mask(
        tissue,
        row_offset + item_ids // HEAD_COUNT,
        item_ids % HEAD_COUNT,
        column_indices,
        dilation_levels,
        segment_levels,
        selected_count,
        column_total,
    )
    dilation_permitted = dilation_permitted.reshape(
        device_rows, HEAD_COUNT, device_columns, selected_count
    )
    query_grid = query_matrix.reshape(device_rows, device_columns, HEAD_COUNT, head_dimension)
    grid_numer, grid_max, grid_sum = dilation_in_grid(
        query_grid, key_grid, value_grid, dilation_permitted
    )
    dilation_numer = grid_numer.reshape(-1, HEAD_COUNT, head_dimension)
    dilation_score_max = grid_max.transpose(0, 2, 1).reshape(-1, HEAD_COUNT)
    dilation_sum = grid_sum.transpose(0, 2, 1).reshape(-1, HEAD_COUNT)
    attended = (
        merge_partials(
            neighbour_numer,
            neighbour_max,
            neighbour_sum,
            dilation_numer,
            dilation_score_max,
            dilation_sum,
        )
        .reshape(-1, model_width)
        .astype(jnp.bfloat16)
    )
    encoded = jnp.dot(attended, output_matrix, preferred_element_type=jnp.float32).astype(
        jnp.bfloat16
    )
    return encoded.reshape(device_rows, device_columns, model_width)


def solution(mesh):
    in_specs = (
        P("row", "col", None),
        P("row", "col", None),
        P("row", "col", None),
        P(),
        P(),
        P(),
        P(),
    )
    out_specs = P("row", "col", None)
    return jax.shard_map(
        per_device, mesh=mesh, in_specs=in_specs, out_specs=out_specs, check_vma=False
    )
```

profile of v0, /device:TPU:56, one launch (start us, length us, event | category | flops | bytes accessed | tf_op | source)
XLA Modules:
  0.0 276.5 jit_solution(2129543870219069759)
XLA Ops:
  2.0 2.7 collective-permute-start.1
  4.7 2.4 collective-permute-start
  7.2 1.9 fusion.111
  9.1 10.0 %fusion.98 = s32[128]{0:T(128)S(1)} fusion(s32[]{:T(128)} %bitcast.62, s32[]{:T(128)} %bitcast.63, s32[]{:T(128)} %bitcast.64, s32[]{:T(128)} %bitcast.65, s32[]{:T(128)} %bitcast.66, s32[]{:T(128)} %bitcast.68, s32[]{:T(128)} %bitcast.67, s32[]{:T(128)} %bitcast.53, s32[]{:T(128)} %bitcast.54, s32[]{:T(128)} %bitcast.55, s32[]{:T(128)} %bitcast.56, ...), kind=kLoop, calls=%fused_computation.190 | loop fusion | flops 5120 | bytes 576 | tf_op jit(solution)/shard_map/shift_left | solution.py:94
  19.3 1.6 reshape.570
  20.9 1.6 reshape.584
  23.2 10.0 %fusion.97 = s32[128]{0:T(128)S(1)} fusion(s32[]{:T(128)} %bitcast.45, s32[]{:T(128)} %bitcast.46, s32[]{:T(128)} %bitcast.47, s32[]{:T(128)} %bitcast.48, s32[]{:T(128)} %bitcast.49, s32[]{:T(128)} %bitcast.51, s32[]{:T(128)} %bitcast.50, s32[]{:T(128)} %bitcast.28, s32[]{:T(128)} %bitcast.30, s32[]{:T(128)} %bitcast.32, s32[]{:T(128)} %bitcast.34, ...), kind=kLoop, calls=%fused_computation.189 | loop fusion | flops 5120 | bytes 576 | tf_op jit(solution)/shard_map/shift_right_arithmetic | solution.py:95
  33.5 65.0 %gather_fusion = s32[8192]{0:T(1024)S(1)} fusion(s32[128,512]{1,0:T(8,128)S(1)} %copy-done.1, s32[8192]{0:T(1024)S(1)} %reshape.613), kind=kCustom, calls=%fused_computation | custom fusion | bytes 131072 | tf_op jit(solution)/shard_map/gather | solution.py:93
  102.8 2.2 and_or_fusion
  105.7 55.9 %all_gather.6 = bf16[8,64,768]{2,0,1:T(8,128)(2,1)S(1)} all-gather(bf16[8,2,768]{2,0,1:T(8,128)(2,1)S(1)} %copy.179), channel_id=1, replica_groups=mesh['row'=16,'col'=32] {'col'}, dimensions={1}, use_global_device_ids=true | all-gather | bytes 811008 | tf_op jit(solution)/shard_map/all_gather | solution.py:177
  162.2 1.6 copy.180
  163.9 2.0 fusion.113
  168.4 3.9 %collective-permute-start.2 = (bf16[24,8,1536]{2,1,0:T(8,128)(2,1)}, bf16[24,8,1536]{2,1,0:T(8,128)(2,1)}, u32[]{:S(2)}, u32[]{:S(2)}) collective-permute-start(bf16[24,8,1536]{2,1,0:T(8,128)(2,1)} %get-tuple-element.28), channel_id=1, source_target_pairs={{0,1},{1,2},{2,3},{3,4},{4,5},{5,6},{6,7},{7,8},{8,9},{9,10},{10,1... | collective-permute-start | bytes 1769480 | tf_op jit(solution)/shard_map/ppermute | solution.py:21
  174.6 1.5 copy.227
  176.0 1.4 copy.225
  183.5 51.7 %all_gather.7 = bf16[8,64,768]{2,0,1:T(8,128)(2,1)S(1)} all-gather(bf16[8,2,768]{2,0,1:T(8,128)(2,1)S(1)} %copy.199), channel_id=1, replica_groups=mesh['row'=16,'col'=32] {'col'}, dimensions={1}, use_global_device_ids=true | all-gather | bytes 811008 | tf_op jit(solution)/shard_map/all_gather | solution.py:178
  235.2 1.6 copy.200
  236.8 2.4 convolution_bitcast_fusion
  240.9 1.7 pad_maximum_fusion
  244.0 1.7 copy.235
  245.7 1.7 copy.234
  247.4 1.7 copy.233
  254.4 1.7 copy.226
  270.4 1.6 fusion.19
  (172 shorter events, 46.2 us)
Async XLA Ops:
  0.0 275.4 %copy-start = (bf16[768,768]{1,0:T(8,128)(2,1)S(1)}, bf16[768,768]{1,0:T(8,128)(2,1)}, u32[]{:S(2)}) copy-start(bf16[768,768]{1,0:T(8,128)(2,1)} %param.16) | copy-start | bytes 3538948
  0.0 22.5 %copy-start.23 = (s32[16]{0:T(128)S(1)}, s32[16]{0:T(128)}, u32[]{:S(2)}) copy-start(s32[16]{0:T(128)} %param.15) | copy-start | bytes 196
  0.0 33.5 %copy-start.1 = (s32[128,512]{1,0:T(8,128)S(1)}, s32[128,512]{1,0:T(8,128)}, u32[]{:S(2)}) copy-start(s32[128,512]{1,0:T(8,128)} %param.13) | copy-start | bytes 786436
  2.0 163.9 %collective-permute-start.1 = (bf16[8,16,1536]{2,1,0:T(8,128)(2,1)S(1)}, bf16[8,16,1536]{2,1,0:T(8,128)(2,1)}, u32[]{:S(2)}, u32[]{:S(2)}) collective-permute-start(bf16[8,16,1536]{2,1,0:T(8,128)(2,1)S(1)} %constant_dynamic-update-slice_fusion), channel_id=1, source_target_pairs={{32,0},{64,32},{96,64},{128,96},{160,128},{192,160},{224,192},{256... | collective-permute-start | bytes 1179656 | tf_op jit(solution)/shard_map/ppermute | solution.py:22
  4.7 161.2 %collective-permute-start = (bf16[8,16,1536]{2,1,0:T(8,128)(2,1)S(1)}, bf16[8,16,1536]{2,1,0:T(8,128)(2,1)}, u32[]{:S(2)}, u32[]{:S(2)}) collective-permute-start(bf16[8,16,1536]{2,1,0:T(8,128)(2,1)S(1)} %constant_dynamic-update-slice_fusion), channel_id=1, source_target_pairs={{0,32},{32,64},{64,96},{96,128},{128,160},{160,192},{192,224},{224... | collective-permute-start | bytes 1179656 | tf_op jit(solution)/shard_map/ppermute | solution.py:21
  33.5 65.1 %copy-start.4 = (bf16[8,16,768]{2,1,0:T(8,128)(2,1)S(1)}, bf16[8,16,768]{2,1,0:T(8,128)(2,1)}, u32[]{:S(2)}) copy-start(bf16[8,16,768]{2,1,0:T(8,128)(2,1)} %param.10) | copy-start | bytes 589828
  33.5 65.9 %copy-start.40 = (pred[8,16]{1,0:T(8,128)(4,1)S(1)}, pred[8,16]{1,0:T(8,128)(4,1)}, u32[]{:S(2)}) copy-start(pred[8,16]{1,0:T(8,128)(4,1)} %constant.110.clone) | copy-start | bytes 388
  101.4 73.2 %copy-start.5 = (s32[8,16,64]{2,1,0:T(8,128)}, s32[8,16,64]{2,1,0:T(8,128)S(1)}, u32[]{:S(2)}) copy-start(s32[8,16,64]{2,1,0:T(8,128)S(1)} %add_select_fusion.1) | copy-start | bytes 98308
  165.9 16.7 %copy-start.7 = (f32[8,16,16]{2,1,0:T(8,128)}, f32[8,16,16]{2,1,0:T(8,128)S(1)}, u32[]{:S(2)}) copy-start(f32[8,16,16]{2,1,0:T(8,128)S(1)} %get-tuple-element.72) | copy-start | bytes 24580
  167.2 10.3 %copy-start.22 = (bf16[128,96]{1,0:T(8,128)(2,1)S(1)}, bf16[128,96]{1,0:T(8,128)(2,1)}, u32[]{:S(2)}) copy-start(bf16[128,96]{1,0:T(8,128)(2,1)} %get-tuple-element.32) | copy-start | bytes 73732
  167.2 11.0 %copy-start.21 = (bf16[128,96]{1,0:T(8,128)(2,1)S(1)}, bf16[128,96]{1,0:T(8,128)(2,1)}, u32[]{:S(2)}) copy-start(bf16[128,96]{1,0:T(8,128)(2,1)} %get-tuple-element.33) | copy-start | bytes 73732
  167.2 11.7 %copy-start.20 = (bf16[128,96]{1,0:T(8,128)(2,1)S(1)}, bf16[128,96]{1,0:T(8,128)(2,1)}, u32[]{:S(2)}) copy-start(bf16[128,96]{1,0:T(8,128)(2,1)} %get-tuple-element.34) | copy-start | bytes 73732
  167.2 12.4 %copy-start.19 = (bf16[128,96]{1,0:T(8,128)(2,1)S(1)}, bf16[128,96]{1,0:T(8,128)(2,1)}, u32[]{:S(2)}) copy-start(bf16[128,96]{1,0:T(8,128)(2,1)} %get-tuple-element.35) | copy-start | bytes 73732
  167.2 13.1 %copy-start.18 = (bf16[128,96]{1,0:T(8,128)(2,1)S(1)}, bf16[128,96]{1,0:T(8,128)(2,1)}, u32[]{:S(2)}) copy-start(bf16[128,96]{1,0:T(8,128)(2,1)} %get-tuple-element.36) | copy-start | bytes 73732
  167.3 14.4 %copy-start.3 = (pred[8,16,24,32]{3,2,1,0:T(8,128)(4,1)S(1)}, pred[8,16,24,32]{3,2,1,0:T(8,128)(4,1)}, u32[]{:S(2)}) copy-start(pred[8,16,24,32]{3,2,1,0:T(8,128)(4,1)} %and_or_fusion) | copy-start | bytes 294916
  167.3 15.2 %copy-start.17 = (bf16[8,2,16,48]{3,2,1,0:T(8,128)(2,1)S(1)}, bf16[8,2,16,48]{3,2,1,0:T(8,128)(2,1)}, u32[]{:S(2)}) copy-start(bf16[8,2,16,48]{3,2,1,0:T(8,128)(2,1)} %get-tuple-element.6) | copy-start | bytes 73732
  168.4 72.5 %collective-permute-start.2 = (bf16[24,8,1536]{2,1,0:T(8,128)(2,1)}, bf16[24,8,1536]{2,1,0:T(8,128)(2,1)}, u32[]{:S(2)}, u32[]{:S(2)}) collective-permute-start(bf16[24,8,1536]{2,1,0:T(8,128)(2,1)} %get-tuple-element.28), channel_id=1, source_target_pairs={{0,1},{1,2},{2,3},{3,4},{4,5},{5,6},{6,7},{7,8},{8,9},{9,10},{10,1... | collective-permute-start | bytes 1769480 | tf_op jit(solution)/shard_map/ppermute | solution.py:21
  172.2 68.7 %collective-permute-start.3 = (bf16[24,8,1536]{2,1,0:T(8,128)(2,1)}, bf16[24,8,1536]{2,1,0:T(8,128)(2,1)}, u32[]{:S(2)}, u32[]{:S(2)}) collective-permute-start(bf16[24,8,1536]{2,1,0:T(8,128)(2,1)} %get-tuple-element.29), channel_id=1, source_target_pairs={{1,0},{2,1},{3,2},{4,3},{5,4},{6,5},{7,6},{8,7},{9,8},{10,9},{11,1... | collective-permute-start | bytes 1769480 | tf_op jit(solution)/shard_map/ppermute | solution.py:22
  253.2 5.8 %copy-start.31 = (bf16[128,96]{0,1:T(8,128)(2,1)S(1)}, bf16[128,96]{0,1:T(8,128)(2,1)}, u32[]{:S(2)}) copy-start(bf16[128,96]{0,1:T(8,128)(2,1)} %copy.213) | copy-start | bytes 73732
  254.4 4.9 %copy-start.30 = (bf16[128,96]{0,1:T(8,128)(2,1)S(1)}, bf16[128,96]{0,1:T(8,128)(2,1)}, u32[]{:S(2)}) copy-start(bf16[128,96]{0,1:T(8,128)(2,1)} %copy.215) | copy-start | bytes 73732
  265.9 4.5 %copy-start.10 = (bf16[768,96]{0,1:T(8,128)(2,1)S(1)}, bf16[768,96]{0,1:T(8,128)(2,1)}, u32[]{:S(2)}) copy-start(bf16[768,96]{0,1:T(8,128)(2,1)} %copy.234) | copy-start | bytes 442372
  266.2 5.8 %copy-start.9 = (bf16[768,96]{0,1:T(8,128)(2,1)S(1)}, bf16[768,96]{0,1:T(8,128)(2,1)}, u32[]{:S(2)}) copy-start(bf16[768,96]{0,1:T(8,128)(2,1)} %copy.235) | copy-start | bytes 442372
  267.1 7.1 %copy-start.32 = (f32[128,16]{0,1:T(8,128)S(1)}, f32[128,16]{0,1:T(8,128)}, u32[]{:S(2)}) copy-start(f32[128,16]{0,1:T(8,128)} %reshape.588) | copy-start | bytes 24580
  268.1 7.3 %copy-start.2 = (f32[128,768]{0,1:T(8,128)S(1)}, f32[128,768]{0,1:T(8,128)}, u32[]{:S(2)}) copy-start(f32[128,768]{0,1:T(8,128)} %copy.202) | copy-start | bytes 1179652
  (21 other events, 44.4 us)
where the time goes:
time: 278 us; the launch traced here: 276 us
  local copies, waits for them, and re-layouts  109 us (39%)
  blocking collectives  108 us (39%)
  other arithmetic  34.9 us (13%)
  matrix products  14.1 us (5%)
  starting transfers between devices  10.2 us (4%)
    gather x1, local copies, waits for them, and re-layouts, dilation_valid_mask(): tissue_keys = tissue[row_indices[:, None], key_columns]  65 us
    all_gather x1, blocking collectives, per_device(): lax.all_gather(key_selected, 'col', axis=1, tiled=True)  55.9 us
    all_gather x1, blocking collectives, per_device(): lax.all_gather(value_selected, 'col', axis=1, tiled=True)  51.7 us
    unnamed x107, local copies, waits for them, and re-layouts  21.9 us
    shift_left x1, other arithmetic, dilation_valid_mask(): jnp.left_shift(jnp.int32(DILATION_MIN), dilation_levels[head_indices])  10 us
    shift_right_arithmetic x1, other arithmetic, dilation_valid_mask(): jnp.right_shift(jnp.int32(column_total), segment_levels[head_indices])  10 us
    ppermute x2, starting transfers between devices, padded_2(): before = lax.ppermute(last, axis, up)  6.23 us
  transfers between devices with their start and end apart: 4, of which 0 were waited for; matrix products, arithmetic and copies ran while one was open for 43% of the time, Pallas kernels for 0%

commit v1 on v0

--- a/solution.py
+++ b/solution.py
@@ -175,7 +175,9 @@
     token_count = device_rows * HEAD_COUNT
     k_all, v_all = (
         lax.all_gather(key_selected, "col", axis=1, tiled=True),
-        lax.all_gather(value_selected, "col", axis=1, tiled=True),
+        jnp.concatenate(
+            lax.all_to_all(jnp.stack([value_selected] * lax.axis_size("col")), "col", 0, 0), axis=1
+        ),
     )
     key_grid = k_all.reshape(device_rows, selected_count, HEAD_COUNT, head_dimension)
     value_grid = v_all.reshape(device_rows, selected_count, HEAD_COUNT, head_dimension)

time: 278 us -> 261 us (0.939)
  blocking collectives: 108 us -> 60 us
  starting transfers between devices: 10.2 us -> 24.1 us
  matrix products: 14.1 us -> 22.7 us
  local copies, waits for them, and re-layouts: 109 us -> 117 us
    all_gather x1 -> x0, blocking collectives: 51.7 us -> none  [per_device(): lax.all_gather(value_selected, 'col', axis=1, tiled=True)]
    all_to_all x0 -> x1, starting transfers between devices: none -> 13.3 us  [per_device(): lax.all_to_all(jnp.stack([value_selected] * lax.axis_size('col')), 'col',...]
    unnamed x107 -> x131, local copies, waits for them, and re-layouts: 21.9 us -> 27.7 us
    another operation x0 -> x4, local copies, waits for them, and re-layouts: none -> 5.6 us  [the longest x1 4.52 us: per_device(): v_all.reshape(device_rows, selected_count, HEAD_COUNT, head_dimension)]
    dot_general x8, matrix products: 4.9 us -> 10.2 us  [window_part(): jnp.einsum('hqk,khd->qhd', exp_terms.astype(jnp.bfloat16), value_grp, pre...]
    all_gather x1, blocking collectives: 55.9 us -> 60 us  [per_device(): lax.all_gather(key_selected, 'col', axis=1, tiled=True)]
  transfers between devices with their start and end apart: 4 -> 5, of which waited for: 0 -> 0; matrix products, arithmetic and copies ran while one was open for 43% -> 62% of each run, Pallas kernels for 0% -> 0%
where the time goes in v1:
time: 261 us; the launch traced here: 258 us
  local copies, waits for them, and re-layouts  117 us (45%)
  blocking collectives  60 us (23%)
  other arithmetic  33.5 us (13%)
  starting transfers between devices  24.1 us (9%)
  matrix products  22.7 us (9%)
    gather x1, local copies, waits for them, and re-layouts, dilation_valid_mask(): tissue_keys = tissue[row_indices[:, None], key_columns]  65 us
    all_gather x1, blocking collectives, per_device(): lax.all_gather(key_selected, 'col', axis=1, tiled=True)  60 us
    unnamed x131, local copies, waits for them, and re-layouts  27.7 us
    all_to_all x1, starting transfers between devices, per_device(): lax.all_to_all(jnp.stack([value_selected] * lax.axis_size('col')), 'col',...  13.3 us
    dot_general x8, matrix products, window_part(): jnp.einsum('hqk,khd->qhd', exp_terms.astype(jnp.bfloat16), value_grp, pre...  10.2 us
    shift_left x1, other arithmetic, dilation_valid_mask(): jnp.left_shift(jnp.int32(DILATION_MIN), dilation_levels[head_indices])  10.1 us
    shift_right_arithmetic x1, other arithmetic, dilation_valid_mask(): jnp.right_shift(jnp.int32(column_total), segment_levels[head_indices])  10.1 us
    ppermute x2, starting transfers between devices, padded_2(): before = lax.ppermute(last, axis, up)  6.86 us
  transfers between devices with their start and end apart: 5, of which 0 were waited for; matrix products, arithmetic and copies ran while one was open for 62% of the time, Pallas kernels for 0%

profile of v1, /device:TPU:56, one launch (start us, length us, event | category | flops | bytes accessed | tf_op | source)
XLA Modules:
  0.0 258.0 jit_solution(6287952241443019224)
XLA Ops:
  2.0 2.7 %collective-permute-start.1 = (bf16[8,16,1536]{2,1,0:T(8,128)(2,1)S(1)}, bf16[8,16,1536]{2,1,0:T(8,128)(2,1)}, u32[]{:S(2)}, u32[]{:S(2)}) collective-permute-start(bf16[8,16,1536]{2,1,0:T(8,128)(2,1)S(1)} %constant_dynamic-update-slice_fusion), channel_id=1, source_target_pairs={{32,0},{64,32},{96,64},{128,96},{160,128},{192,160},{224,192},{256... | collective-permute-start | bytes 1179656 | tf_op jit(solution)/shard_map/ppermute | solution.py:22
  4.7 2.4 collective-permute-start
  12.4 13.3 %all-to-all-start = ((bf16[32,8,2,768]{3,1,2,0:T(8,128)(2,1)}), bf16[32,8,2,768]{3,1,2,0:T(8,128)(2,1)}, u32[]{:S(2)}, u32[]{:S(2)}) async-start(bf16[32,8,2,768]{3,1,2,0:T(8,128)(2,1)} %stack.3), calls=%async_computation | async-start | bytes 1572864 | tf_op jit(solution)/shard_map/all_to_all | solution.py:179
  26.5 10.1 %fusion.103 = s32[128]{0:T(128)S(1)} fusion(s32[]{:T(128)} %bitcast.62, s32[]{:T(128)} %bitcast.63, s32[]{:T(128)} %bitcast.64, s32[]{:T(128)} %bitcast.65, s32[]{:T(128)} %bitcast.66, s32[]{:T(128)} %bitcast.68, s32[]{:T(128)} %bitcast.67, s32[]{:T(128)} %bitcast.53, s32[]{:T(128)} %bitcast.54, s32[]{:T(128)} %bitcast.55, s32[]{:T(128)} %bitcast.56, ...), kind=kLoop, calls=%fused_computation.192 | loop fusion | flops 5120 | bytes 576 | tf_op jit(solution)/shard_map/shift_left | solution.py:94
  37.6 10.1 %fusion.102 = s32[128]{0:T(128)S(1)} fusion(s32[]{:T(128)} %bitcast.45, s32[]{:T(128)} %bitcast.46, s32[]{:T(128)} %bitcast.47, s32[]{:T(128)} %bitcast.48, s32[]{:T(128)} %bitcast.49, s32[]{:T(128)} %bitcast.51, s32[]{:T(128)} %bitcast.50, s32[]{:T(128)} %bitcast.28, s32[]{:T(128)} %bitcast.30, s32[]{:T(128)} %bitcast.32, s32[]{:T(128)} %bitcast.34, ...), kind=kLoop, calls=%fused_computation.191 | loop fusion | flops 5120 | bytes 576 | tf_op jit(solution)/shard_map/shift_right_arithmetic | solution.py:95
  48.0 65.0 %gather_fusion = s32[8192]{0:T(1024)S(1)} fusion(s32[128,512]{1,0:T(8,128)S(1)} %copy-done.1, s32[8192]{0:T(1024)S(1)} %reshape.611), kind=kCustom, calls=%fused_computation | custom fusion | bytes 131072 | tf_op jit(solution)/shard_map/gather | solution.py:93
  119.2 4.5 %collective-permute-start.2 = (bf16[24,8,1536]{2,1,0:T(8,128)(2,1)}, bf16[24,8,1536]{2,1,0:T(8,128)(2,1)}, u32[]{:S(2)}, u32[]{:S(2)}) collective-permute-start(bf16[24,8,1536]{2,1,0:T(8,128)(2,1)} %get-tuple-element.28), channel_id=1, source_target_pairs={{0,1},{1,2},{2,3},{3,4},{4,5},{5,6},{6,7},{7,8},{8,9},{9,10},{10,1... | collective-permute-start | bytes 1769480 | tf_op jit(solution)/shard_map/ppermute | solution.py:21
  125.0 60.0 %all_gather.3 = bf16[8,64,768]{2,0,1:T(8,128)(2,1)S(1)} all-gather(bf16[8,2,768]{2,0,1:T(8,128)(2,1)S(1)} %copy.181), channel_id=1, replica_groups=mesh['row'=16,'col'=32] {'col'}, dimensions={1}, use_global_device_ids=true | all-gather | bytes 811008 | tf_op jit(solution)/shard_map/all_gather | solution.py:177
  193.0 1.9 copy.182
  194.9 2.0 fusion.118
  199.4 1.7 pad_maximum_fusion
  204.5 1.7 copy.231
  206.2 1.7 copy.230
  212.7 1.7 copy.222
  214.4 1.7 copy.220
  231.5 1.7 copy.237
  233.3 1.7 copy.236
  235.0 1.7 copy.235
  238.3 1.9 fusion.27
  240.3 2.1 fusion.26
  242.4 1.8 fusion.25
  245.1 1.8 fusion.23
  247.9 4.5 %reshape_reshape.3 = bf16[8,64,16,48]{3,2,0,1:T(8,128)(2,1)} reshape(bf16[8,32,2,768]{3,0,2,1:T(8,128)(2,1)} %bitcast.92) | data formatting | bytes 1572864 | tf_op jit(solution)/shard_map/reshape;reshape | solution.py:183
  252.5 3.4 %fusion.2 = f32[8,16,16,48]{3,1,2,0:T(8,128)S(1)} fusion(bf16[8,64,16,48]{3,2,0,1:T(8,128)(2,1)} %reshape_reshape.3, f32[8,16,16,64]{3,2,1,0:T(8,128)S(1)} %get-tuple-element.73, f32[8,16,16]{2,1,0:T(8,128)S(1)} %copy-done.13, s32[8,16,16]{2,1,0:T(8,128)S(1)} %copy-done.11, s32[8,16,64]{2,1,0:T(8,128)S(1)} %copy-done.9, pred[8,16,64]{2,1,0:T(8,128)(4,1)S(1)} %copy-done.26), kind=kOutput, calls=%fused_computation.5 | convolution fusion | flops 13238272 | bytes 1761280 | tf_op jit(solution)/shard_map/rhcs,rshw->rchw/dot_general | solution.py:112
  (198 shorter events, 55.8 us)
Async XLA Ops:
  0.0 256.9 %copy-start = (bf16[768,768]{1,0:T(8,128)(2,1)S(1)}, bf16[768,768]{1,0:T(8,128)(2,1)}, u32[]{:S(2)}) copy-start(bf16[768,768]{1,0:T(8,128)(2,1)} %param.16) | copy-start | bytes 3538948
  2.0 114.9 %collective-permute-start.1 = (bf16[8,16,1536]{2,1,0:T(8,128)(2,1)S(1)}, bf16[8,16,1536]{2,1,0:T(8,128)(2,1)}, u32[]{:S(2)}, u32[]{:S(2)}) collective-permute-start(bf16[8,16,1536]{2,1,0:T(8,128)(2,1)S(1)} %constant_dynamic-update-slice_fusion), channel_id=1, source_target_pairs={{32,0},{64,32},{96,64},{128,96},{160,128},{192,160},{224,192},{256... | collective-permute-start | bytes 1179656 | tf_op jit(solution)/shard_map/ppermute | solution.py:22
  4.7 112.2 %collective-permute-start = (bf16[8,16,1536]{2,1,0:T(8,128)(2,1)S(1)}, bf16[8,16,1536]{2,1,0:T(8,128)(2,1)}, u32[]{:S(2)}, u32[]{:S(2)}) collective-permute-start(bf16[8,16,1536]{2,1,0:T(8,128)(2,1)S(1)} %constant_dynamic-update-slice_fusion), channel_id=1, source_target_pairs={{0,32},{32,64},{64,96},{96,128},{128,160},{160,192},{192,224},{224... | collective-permute-start | bytes 1179656 | tf_op jit(solution)/shard_map/ppermute | solution.py:21
  8.7 17.1 %copy-start.27 = (s32[16]{0:T(128)S(1)}, s32[16]{0:T(128)}, u32[]{:S(2)}) copy-start(s32[16]{0:T(128)} %param.14) | copy-start | bytes 196
  8.7 28.2 %copy-start.28 = (s32[16]{0:T(128)S(1)}, s32[16]{0:T(128)}, u32[]{:S(2)}) copy-start(s32[16]{0:T(128)} %param.15) | copy-start | bytes 196
  8.7 39.3 %copy-start.1 = (s32[128,512]{1,0:T(8,128)S(1)}, s32[128,512]{1,0:T(8,128)}, u32[]{:S(2)}) copy-start(s32[128,512]{1,0:T(8,128)} %param.13) | copy-start | bytes 786436
  12.4 235.5 %all-to-all-start = ((bf16[32,8,2,768]{3,1,2,0:T(8,128)(2,1)}), bf16[32,8,2,768]{3,1,2,0:T(8,128)(2,1)}, u32[]{:S(2)}, u32[]{:S(2)}) async-start(bf16[32,8,2,768]{3,1,2,0:T(8,128)(2,1)} %stack.3), calls=%async_computation | async-start | bytes 1572864 | tf_op jit(solution)/shard_map/all_to_all | solution.py:179
  48.0 65.1 %copy-start.7 = (bf16[8,16,768]{2,1,0:T(8,128)(2,1)S(1)}, bf16[8,16,768]{2,1,0:T(8,128)(2,1)}, u32[]{:S(2)}) copy-start(bf16[8,16,768]{2,1,0:T(8,128)(2,1)} %param.10) | copy-start | bytes 589828
  48.0 67.8 %copy-start.23 = (pred[8,16,24,32]{3,2,1,0:T(8,128)(4,1)S(1)}, pred[8,16,24,32]{3,2,1,0:T(8,128)(4,1)}, u32[]{:S(2)}) copy-start(pred[8,16,24,32]{3,2,1,0:T(8,128)(4,1)} %constant.109.clone) | copy-start | bytes 294916
  48.0 67.8 %copy-start.24 = (pred[8,16,24,32]{3,2,1,0:T(8,128)(4,1)S(1)}, pred[8,16,24,32]{3,2,1,0:T(8,128)(4,1)}, u32[]{:S(2)}) copy-start(pred[8,16,24,32]{3,2,1,0:T(8,128)(4,1)} %constant.108.clone) | copy-start | bytes 294916
  114.0 83.6 %copy-start.8 = (s32[8,16,64]{2,1,0:T(8,128)}, s32[8,16,64]{2,1,0:T(8,128)S(1)}, u32[]{:S(2)}) copy-start(s32[8,16,64]{2,1,0:T(8,128)S(1)} %add_select_fusion.1) | copy-start | bytes 98308
  114.8 82.9 %copy-start.10 = (s32[8,16,16]{2,1,0:T(8,128)}, s32[8,16,16]{2,1,0:T(8,128)S(1)}, u32[]{:S(2)}) copy-start(s32[8,16,16]{2,1,0:T(8,128)S(1)} %add_select_fusion) | copy-start | bytes 24580
  115.5 82.1 %copy-start.25 = (pred[8,16,64]{2,1,0:T(8,128)(4,1)}, pred[8,16,64]{2,1,0:T(8,128)(4,1)S(1)}, u32[]{:S(2)}) copy-start(pred[8,16,64]{2,1,0:T(8,128)(4,1)S(1)} %fusion.84) | copy-start | bytes 24580
  119.2 80.2 %collective-permute-start.2 = (bf16[24,8,1536]{2,1,0:T(8,128)(2,1)}, bf16[24,8,1536]{2,1,0:T(8,128)(2,1)}, u32[]{:S(2)}, u32[]{:S(2)}) collective-permute-start(bf16[24,8,1536]{2,1,0:T(8,128)(2,1)} %get-tuple-element.28), channel_id=1, source_target_pairs={{0,1},{1,2},{2,3},{3,4},{4,5},{5,6},{6,7},{7,8},{8,9},{9,10},{10,1... | collective-permute-start | bytes 1769480 | tf_op jit(solution)/shard_map/ppermute | solution.py:21
  123.7 75.7 %collective-permute-start.3 = (bf16[24,8,1536]{2,1,0:T(8,128)(2,1)}, bf16[24,8,1536]{2,1,0:T(8,128)(2,1)}, u32[]{:S(2)}, u32[]{:S(2)}) collective-permute-start(bf16[24,8,1536]{2,1,0:T(8,128)(2,1)} %get-tuple-element.29), channel_id=1, source_target_pairs={{1,0},{2,1},{3,2},{4,3},{5,4},{6,5},{7,6},{8,7},{9,8},{10,9},{11,1... | collective-permute-start | bytes 1769480 | tf_op jit(solution)/shard_map/ppermute | solution.py:22
  209.5 8.8 %copy-start.16 = (bf16[768,96]{1,0:T(8,128)(2,1)S(1)}, bf16[768,96]{1,0:T(8,128)(2,1)}, u32[]{:S(2)}) copy-start(bf16[768,96]{1,0:T(8,128)(2,1)} %get-tuple-element.19) | copy-start | bytes 442372
  228.1 8.6 %copy-start.15 = (bf16[768,96]{1,0:T(8,128)(2,1)S(1)}, bf16[768,96]{1,0:T(8,128)(2,1)}, u32[]{:S(2)}) copy-start(bf16[768,96]{1,0:T(8,128)(2,1)} %get-tuple-element.23) | copy-start | bytes 442372
  228.1 9.4 %copy-start.14 = (bf16[768,96]{1,0:T(8,128)(2,1)S(1)}, bf16[768,96]{1,0:T(8,128)(2,1)}, u32[]{:S(2)}) copy-start(bf16[768,96]{1,0:T(8,128)(2,1)} %get-tuple-element.24) | copy-start | bytes 442372
  228.4 11.9 %copy-start.40 = (f32[2,128]{1,0:T(2,128)S(1)}, f32[2,128]{1,0:T(2,128)}, u32[]{:S(2)}) copy-start(f32[2,128]{1,0:T(2,128)} %copy-done.39) | copy-start | bytes 3076
  229.2 13.2 %copy-start.42 = (f32[2,128]{1,0:T(2,128)S(1)}, f32[2,128]{1,0:T(2,128)}, u32[]{:S(2)}) copy-start(f32[2,128]{1,0:T(2,128)} %copy-done.41) | copy-start | bytes 3076
  236.7 8.4 %copy-start.44 = (f32[2,128]{1,0:T(2,128)S(1)}, f32[2,128]{1,0:T(2,128)}, u32[]{:S(2)}) copy-start(f32[2,128]{1,0:T(2,128)} %copy-done.43) | copy-start | bytes 3076
  245.0 7.4 %copy-start.11 = (s32[8,16,16]{2,1,0:T(8,128)S(1)}, s32[8,16,16]{2,1,0:T(8,128)}, u32[]{:S(2)}) copy-start(s32[8,16,16]{2,1,0:T(8,128)} %copy-done.10) | copy-start | bytes 24580
  245.0 7.4 %copy-start.13 = (f32[8,16,16]{2,1,0:T(8,128)S(1)}, f32[8,16,16]{2,1,0:T(8,128)}, u32[]{:S(2)}) copy-start(f32[8,16,16]{2,1,0:T(8,128)} %copy-done.12) | copy-start | bytes 24580
  245.0 7.4 %copy-start.26 = (pred[8,16,64]{2,1,0:T(8,128)(4,1)S(1)}, pred[8,16,64]{2,1,0:T(8,128)(4,1)}, u32[]{:S(2)}) copy-start(pred[8,16,64]{2,1,0:T(8,128)(4,1)} %copy-done.25) | copy-start | bytes 24580
  (34 other events, 114.3 us)
